TPU v7x, 128 devices: a whole 4x4x4 slice. The times are simulated.
128 devices in a mesh: phrase: 16 (over y, z_lo, core), vocab: 8 (over x, z_hi).
Axes of the slice: x: 4, y: 4, z: 4 (z_hi: 2, z_lo: 2; z = z_hi * 2 + z_lo), core: 2. Of those that a mesh axis runs over, the one named last changes fastest.
Arguments:
- frames: bfloat16 [1536, 1024], P(('phrase', 'vocab'))
- frame_lens: int32 [4], replicated, may hold values from 192 to 384, as said below
- labels: int32 [4, 64], replicated, may hold values from 1 to 4095
- label_lens: int32 [4], replicated, may hold values from 16 to 63, as said below
- phrase_ids: int32 [65536, 8], P(('phrase', 'vocab')), may hold values from 0 to 4095
- phrase_lens: int32 [65536], P(('phrase', 'vocab')), may hold values from 1 to 8
- phrase_table: bfloat16 [4096, 512], replicated, may hold values from -6 to 6
- phrase_w: bfloat16 [512, 512], replicated, may hold values from -0.25 to 0.25
- key_w: bfloat16 [512, 512], replicated, may hold values from -0.25 to 0.25
- value_w: bfloat16 [512, 512], replicated, may hold values from -0.25 to 0.25
- query_w: bfloat16 [1024, 512], replicated, may hold values from -0.9375 to 0.9375
- context_w: bfloat16 [512, 1024], replicated, may hold values from -0.25 to 0.25
- joint_enc_w: bfloat16 [1024, 640], replicated, may hold values from -0.1875 to 0.1875
- pred_table: bfloat16 [4096, 640], replicated, may hold values from -6 to 6
- pred_w: bfloat16 [640, 640], replicated, may hold values from -0.25 to 0.25
- out_w: bfloat16 [640, 4096], P(None, 'vocab')
Outputs:
- blank_logp: float32 [1536, 64], P('phrase', 'vocab')
- label_logp: float32 [1536, 64], P('phrase', 'vocab')
Inputs may be any that keep to these rules, and one draw needn't show every extreme that they name: `frame_lens`: some utterance has exactly 384 frames. `label_lens`: some utterance has exactly 63 labels.
All inputs are finite; a program needn't handle non-finite values.
Results may differ from a plain program's by a relative error of at most 0.0034.
Values may be sent and summed in bfloat16 or wider, within the bound.
No kernel may reach another device: no remote copies, remote signals or barrier semaphores. Data moves between devices by JAX's collectives and lax.ppermute only.
A program may use at most 128 MiB of HBM per device.

v0:
```python
import math
import jax
import jax.numpy as jnp
from jax import lax
from jax.sharding import PartitionSpec as P

HEADS = 4


def encode_local(ids, lens, phrase_table, phrase_w):
    emb = phrase_table[ids]
    mask = (jnp.arange(ids.shape[1], dtype=jnp.int32)[None, :] < lens[:, None]).astype(jnp.bfloat16)
    summed = jnp.einsum("npe,np->ne", emb, mask, preferred_element_type=jnp.float32)
    mean = (summed / lens[:, None].astype(jnp.float32)).astype(jnp.bfloat16)
    return jnp.tanh(jnp.dot(mean, phrase_w, preferred_element_type=jnp.float32)).astype(
        jnp.bfloat16
    )


def block_sums(asked, keys, values, blocks):
    head_size = keys.shape[1] // HEADS
    query_heads = asked.reshape(asked.shape[0], HEADS, head_size)
    key_heads = keys.reshape(keys.shape[0], HEADS, head_size)
    scores = jnp.einsum("fhd,phd->fhp", query_heads, key_heads, preferred_element_type=jnp.float32)
    scores = (scores * (1.0 / math.sqrt(head_size))).reshape(
        asked.shape[0], HEADS, blocks, keys.shape[0] // blocks
    )
    block_peak = jnp.max(scores, -1)
    weights = jnp.exp(scores - block_peak[..., None]).astype(jnp.bfloat16)
    block_total = jnp.sum(weights, -1, dtype=jnp.float32)
    value_heads = values.reshape(blocks, values.shape[0] // blocks, HEADS, head_size)
    block_numer = jnp.einsum(
        "fhbp,bphd->fhbd", weights, value_heads, preferred_element_type=jnp.float32
    )
    return (block_peak, block_total, block_numer)


def rescale(block_peak, block_total, block_numer, peak):
    factor = jnp.exp(block_peak - peak[..., None])
    return (jnp.sum(block_total * factor, -1), jnp.sum(block_numer * factor[..., None], 2))


def local(
    frames,
    frame_lens,
    labels,
    label_lens,
    phrase_ids,
    phrase_lens,
    phrase_table,
    phrase_w,
    key_w,
    value_w,
    query_w,
    context_w,
    joint_enc_w,
    pred_table,
    pred_w,
    out_w,
):
    phrase_vec = encode_local(phrase_ids, phrase_lens, phrase_table, phrase_w)
    keys = jnp.dot(phrase_vec, key_w, preferred_element_type=jnp.float32).astype(jnp.bfloat16)
    values = jnp.dot(phrase_vec, value_w, preferred_element_type=jnp.float32).astype(jnp.bfloat16)
    queries = jnp.dot(frames, query_w, preferred_element_type=jnp.float32).astype(jnp.bfloat16)
    asked = lax.all_gather(queries, ("phrase", "vocab"), axis=0, tiled=True)
    block_peak, block_total, block_numer = block_sums(asked, keys, values, 1)
    peak = lax.pmax(jnp.max(block_peak, -1), ("phrase", "vocab"))
    total, numer = rescale(block_peak, block_total, block_numer, peak)
    total, numer = (
        lax.psum_scatter(total, ("phrase", "vocab"), scatter_dimension=0, tiled=True),
        lax.psum_scatter(numer, ("phrase", "vocab"), scatter_dimension=0, tiled=True),
    )
    context = (numer / total[..., None]).reshape(frames.shape[0], -1).astype(jnp.bfloat16)
    biased = (
        frames.astype(jnp.float32) + jnp.dot(context, context_w, preferred_element_type=jnp.float32)
    ).astype(jnp.bfloat16)
    joint_rows = jnp.dot(biased, joint_enc_w, preferred_element_type=jnp.float32).astype(
        jnp.bfloat16
    )
    joint_all = lax.all_gather(joint_rows, "vocab", axis=0, tiled=True)
    n_vocab = lax.axis_size("vocab")
    vocab_index = lax.axis_index("vocab")
    utts, positions = labels.shape
    own = positions // n_vocab
    width = pred_w.shape[0]
    own_labels = lax.dynamic_slice_in_dim(labels, vocab_index * own, own, 1)
    step_rows = (
        jnp.dot(pred_table[own_labels.reshape(-1)], pred_w, preferred_element_type=jnp.float32)
        .astype(jnp.bfloat16)
        .reshape(utts, own, width)
    )
    step_all = lax.all_gather(step_rows, "vocab", axis=1, tiled=True)
    blank_row = jnp.dot(pred_table[0:1], pred_w, preferred_element_type=jnp.float32).astype(
        jnp.bfloat16
    )
    predictor = jnp.concatenate(
        [jnp.broadcast_to(blank_row[None], (utts, 1, width)), step_all[:, :-1]], 1
    )
    frames_dev = joint_all.shape[0]
    tlen = frames_dev * lax.axis_size("phrase") // utts
    global_index = lax.axis_index("phrase") * frames_dev + jnp.arange(frames_dev, dtype=jnp.int32)
    owner = global_index // tlen
    moment = global_index % tlen
    member = owner[:, None] == jnp.arange(utts, dtype=jnp.int32)[None, :]
    pred_sel = jnp.einsum(
        "fb,buh->fuh", member.astype(jnp.bfloat16), predictor, preferred_element_type=jnp.float32
    )
    joint_in = (
        jnp.tanh(joint_all[:, None, :].astype(jnp.float32) + pred_sel)
        .astype(jnp.bfloat16)
        .reshape(-1, width)
    )
    logits = jnp.dot(joint_in, out_w, preferred_element_type=jnp.float32)
    cols = out_w.shape[1]
    row_labels = jnp.sum(jnp.where(member[:, :, None], labels[None, :, :], 0), 1)
    column = vocab_index * cols + jnp.arange(cols, dtype=jnp.int32)
    label_part = jnp.sum(
        jnp.where(column[None, :] == row_labels.reshape(-1, 1), logits, 0.0), -1
    ).reshape(frames_dev, positions)
    blank_part = jnp.where(vocab_index == 0, logits[:, 0], 0.0).reshape(frames_dev, positions)
    start_own = vocab_index * own
    peak_rows = lax.pmax(jnp.max(logits, -1), "vocab")
    total_part = jnp.sum(jnp.exp(logits - peak_rows[:, None]), -1).reshape(frames_dev, positions)
    peak_own = lax.dynamic_slice_in_dim(peak_rows.reshape(frames_dev, positions), start_own, own, 1)
    total_every = lax.psum(total_part, "vocab")
    total_own = lax.dynamic_slice_in_dim(total_every, start_own, own, 1)
    blank_own, label_own = (
        lax.psum_scatter(blank_part, "vocab", scatter_dimension=1, tiled=True),
        lax.psum_scatter(label_part, "vocab", scatter_dimension=1, tiled=True),
    )
    norm = peak_own + jnp.log(total_own)
    positions_own = start_own + jnp.arange(own, dtype=jnp.int32)
    frame_len = jnp.sum(jnp.where(member, frame_lens[None, :], 0), 1)
    label_len = jnp.sum(jnp.where(member, label_lens[None, :], 0), 1)
    live = (moment < frame_len)[:, None]
    blank_out = jnp.where(
        live & (positions_own[None, :] <= label_len[:, None]), blank_own - norm, 0.0
    )
    label_out = jnp.where(
        live & (positions_own[None, :] < label_len[:, None]), label_own - norm, 0.0
    )
    return (blank_out, label_out)


def solution(mesh):
    in_specs = (
        P(("phrase", "vocab"), None),
        P(),
        P(),
        P(),
        P(("phrase", "vocab"), None),
        P(("phrase", "vocab")),
        P(),
        P(),
        P(),
        P(),
        P(),
        P(),
        P(),
        P(),
        P(),
        P(None, "vocab"),
    )
    out_specs = (P("phrase", "vocab"), P("phrase", "vocab"))
    return jax.shard_map(local, mesh=mesh, in_specs=in_specs, out_specs=out_specs, check_vma=False)
```

profile of v0, /device:TPU:0, one launch (start us, length us, event | category | flops | bytes accessed | tf_op | source)
XLA Modules:
  0.0 752.5 jit_solution(592532760997151571)
XLA Ops:
  7.2 2.2 fusion.14
  9.5 0.7 compare_select_fusion
  10.4 0.2 reshape.181
  10.5 0.7 convert_element_type.59
  11.2 0.8 constant_dynamic-slice_fusion.1
  12.0 20.2 %gather_fusion = bf16[4096,512]{1,0:T(8,128)(2,1)} fusion(bf16[4096,512]{1,0:T(8,128)(2,1)} %param.22, s32[4096]{0:T(1024)S(1)} %broadcast_clamp_fusion), kind=kCustom, calls=%fused_computation | custom fusion | bytes 8404992 | tf_op jit(solution)/shard_map/gather | solution.py:11
  32.4 3.5 fusion.2
  35.9 0.5 fusion.8
  36.4 0.5 convolution_convert_fusion
  36.9 1.3 convolution_convert_fusion.1
  38.2 274.2 %all-gather.4.cloned.1.call-done = bf16[128,12,512]{2,1,0:T(8,128)(2,1)} async-done(((bf16[1,12,512]{2,1,0:T(8,128)(2,1)}), bf16[128,12,512]{2,1,0:T(8,128)(2,1)}) %all-gather.4.cloned.1.call-update) | async-done | bytes 1572880 | tf_op jit(solution)/shard_map/all_gather | solution.py:65
  312.4 3.2 reshape.171
  315.6 6.4 bitcast_reduce_fusion
  322.1 66.9 %pmax.14 = f32[1536,4]{0,1:T(4,128)S(1)} all-reduce(f32[1536,4]{0,1:T(4,128)S(1)} %get-tuple-element.19), channel_id=1, replica_groups=mesh['phrase'=16,'vocab'=8] {'phrase','vocab'}, use_global_device_ids=true, to_apply=%region_3.0 | all-reduce | flops 6144 | bytes 49152 | tf_op jit(solution)/shard_map/pmax | solution.py:67
  389.0 6.8 convert_reduce_fusion
  395.8 0.6 fusion.37
  396.4 0.7 copy-done.1
  397.2 5.0 fusion.5
  402.2 5.0 copy.48
  407.2 0.2 all-reduce.10.cloned.1.call-start
  407.5 3.8 gather_fusion.1
  411.3 0.2 fusion.10
  411.6 35.0 %all_gather.11 = bf16[4,64,640]{2,0,1:T(4,128)(2,1)S(1)} all-gather(bf16[4,8,640]{2,0,1:T(4,128)(2,1)S(1)} %copy.50), channel_id=1, replica_groups=mesh['phrase'=16,'vocab'=8] {'vocab'}, dimensions={1}, use_global_device_ids=true | all-gather | bytes 368640 | tf_op jit(solution)/shard_map/all_gather | solution.py:92
  446.8 0.5 copy-done.10
  447.3 0.7 select_reduce_fusion.1
  448.0 0.8 copy.52
  448.8 0.7 eq.42
  449.5 1.2 dynamic-slice.2
  451.4 0.8 select_reduce_fusion.3
  452.2 0.9 convolution_reduce_fusion
  453.1 63.0 %all-reduce.1 = f32[1536,4]{0,1:T(4,128)S(1)} all-reduce(f32[1536,4]{0,1:T(4,128)} %get-tuple-element.15), channel_id=3, replica_groups=mesh['phrase'=16,'vocab'=8] {'phrase','vocab'}, use_global_device_ids=true, to_apply=%region_6.0.clone | all-reduce | flops 6144 | bytes 49152
  516.3 42.6 %all-reduce.8.cloned.1.call-done = f32[1536,4,128]{2,1,0:T(4,128)} async-done(((f32[1536,4,128]{2,1,0:T(4,128)}), f32[1536,4,128]{2,1,0:T(4,128)}) %all-reduce.8.cloned.1.call-update) | async-done | bytes 3145744
  558.9 0.8 fusion.28
  559.8 1.2 fusion.13
  561.0 34.2 %all-gather.1 = bf16[8,12,640]{2,1,0:T(8,128)(2,1)S(1)} all-gather(bf16[1,12,640]{2,1,0:T(8,128)(2,1)S(1)} %fusion.13), channel_id=1, replica_groups=mesh['phrase'=16,'vocab'=8] {'vocab'}, dimensions={0}, use_global_device_ids=true | all-gather | bytes 138240 | tf_op jit(solution)/shard_map/all_gather | solution.py:80
  595.3 3.6 tanh_convert_fusion
  598.9 6.0 copy.51
  605.0 11.2 %fusion.38 = (f32[6144]{0:T(1024)S(1)}, f32[6144,512]{0,1:T(8,128)}) fusion(bf16[6144,640]{1,0:T(8,128)(2,1)} %bitcast.74, bf16[640,512]{1,0:T(8,128)(2,1)S(1)} %copy-done.11), kind=kOutput, calls=%fused_computation.75 | convolution fusion | flops 4029671424 | bytes 21127168 | tf_op jit(solution)/shard_map/dot_general | solution.py:113
  616.2 40.3 %pmax.15 = f32[6144]{0:T(1024)S(1)} all-reduce(f32[6144]{0:T(1024)S(1)} %get-tuple-element.21), channel_id=1, replica_groups=mesh['phrase'=16,'vocab'=8] {'vocab'}, use_global_device_ids=true, to_apply=%region_9.10 | all-reduce | flops 6144 | bytes 49152 | tf_op jit(solution)/shard_map/pmax | solution.py:122
  656.6 6.5 select_reduce_fusion
  663.1 0.7 reshape.177
  663.8 0.7 reshape.178
  664.5 1.0 fusion.27
  665.5 0.7 select_n.81
  666.3 77.4 %all-reduce.10.cloned.1.call-done = (f32[96,64]{1,0:T(8,128)}, f32[96,64]{1,0:T(8,128)}, f32[96,64]{1,0:T(8,128)}) async-done(((f32[96,64]{1,0:T(8,128)}, f32[96,64]{1,0:T(8,128)}, f32[96,64]{1,0:T(8,128)}), (f32[96,64]{1,0:T(8,128)}, f32[96,64]{1,0:T(8,128)}, f32[96,64]{1,0:T(8,128)})) %all-reduce.10.cloned.1.call-update) | async-done | bytes 73744
  743.7 1.0 fusion.25
  744.7 0.7 copy.53
  745.3 0.7 copy.54
  (49 shorter events, 1.0 us)
Async XLA Ops:
  7.2 552.6 %copy-start = (bf16[1024,640]{1,0:T(8,128)(2,1)S(1)}, bf16[1024,640]{1,0:T(8,128)(2,1)}, u32[]{:S(2)}) copy-start(bf16[1024,640]{1,0:T(8,128)(2,1)} %param.28) | copy-start | bytes 3932164
  7.2 305.3 %all-gather.4.cloned.1.call-start = ((), (), s32[]{:S(2)}) async-start(), calls=%async_computation | async-start | bytes 2113536 | tf_op jit(solution)/shard_map/all_gather | solution.py:65
  9.4 549.5 %all-reduce.8.cloned.1.call-start = ((), (), s32[]{:S(2)}) async-start(), calls=%async_computation.1 | async-start | bytes 6291456
  12.0 20.2 %copy-start.7 = (s32[512]{0:T(512)S(1)}, s32[512]{0:T(512)}, u32[]{:S(2)}) copy-start(s32[512]{0:T(512)} %param.21) | copy-start | bytes 6148
  12.0 23.9 %copy-start.12 = (bf16[512,512]{1,0:T(8,128)(2,1)S(1)}, bf16[512,512]{1,0:T(8,128)(2,1)}, u32[]{:S(2)}) copy-start(bf16[512,512]{1,0:T(8,128)(2,1)} %param.23) | copy-start | bytes 1572868
  32.2 4.2 copy-start.4
  32.2 4.7 copy-start.5
  389.0 8.2 %copy-start.1 = (f32[4,512,1536]{2,1,0:T(8,128)S(1)}, f32[4,512,1536]{2,1,0:T(8,128)}, u32[]{:S(2)}) copy-start(f32[4,512,1536]{2,1,0:T(8,128)} %get-tuple-element.20) | copy-start | bytes 37748740
  402.2 9.1 %copy-start.2 = (bf16[640,640]{1,0:T(8,128)(2,1)S(1)}, bf16[640,640]{1,0:T(8,128)(2,1)}, u32[]{:S(2)}) copy-start(bf16[640,640]{1,0:T(8,128)(2,1)} %param.30) | copy-start | bytes 2457604
  402.2 45.1 %copy-start.8 = (s32[4,64]{1,0:T(4,128)S(1)}, s32[4,64]{1,0:T(4,128)}, u32[]{:S(2)}) copy-start(s32[4,64]{1,0:T(4,128)} %param.18) | copy-start | bytes 3076
  402.2 49.2 %copy-start.9 = (s32[4]{0:T(128)S(1)}, s32[4]{0:T(128)}, u32[]{:S(2)}) copy-start(s32[4]{0:T(128)} %param.17) | copy-start | bytes 52
  402.2 157.6 %copy-start.3 = (bf16[512,1024]{1,0:T(8,128)(2,1)S(1)}, bf16[512,1024]{1,0:T(8,128)(2,1)}, u32[]{:S(2)}) copy-start(bf16[512,1024]{1,0:T(8,128)(2,1)} %param.27) | copy-start | bytes 3145732
  407.2 336.4 %all-reduce.10.cloned.1.call-start = ((), (), s32[]{:S(2)}) async-start(), calls=%async_computation.2 | async-start | bytes 294912
  446.8 0.5 copy-start.10
  598.9 6.0 copy-start.11
  605.0 51.6 %copy-start.6 = (s32[6144]{0:T(1024)S(1)}, s32[6144]{0:T(1024)}, u32[]{:S(2)}) copy-start(s32[6144]{0:T(1024)} %eq.42) | copy-start | bytes 73732
Sparse Core Ops, SparseCore 0:
  9.7 302.6 all-gather.3
  407.4 151.5 all-reduce.7
  666.3 77.2 all-reduce.9
where the time goes:
time: 753 us
  waiting for transfers between devices  394 us (52%)
  blocking collectives  240 us (32%)
  local copies, waits for them, and re-layouts  47.1 us (6%)
  matrix products  36.7 us (5%)
  other arithmetic  19.8 us (3%)
  between operations  14.7 us (2%)
    all_gather x1, waiting for transfers between devices, local(): asked = lax.all_gather(queries, ('phrase', 'vocab'), axis=0, tiled=True)  274 us
    unnamed x5, waiting for transfers between devices  120 us
    pmax x1, blocking collectives, local(): peak = lax.pmax(jnp.max(block_peak, -1), ('phrase', 'vocab'))  66.9 us
    unnamed x1, blocking collectives  63 us
    pmax x1, blocking collectives, local(): peak_rows = lax.pmax(jnp.max(logits, -1), 'vocab')  40.3 us
    all_gather x1, blocking collectives, local(): step_all = lax.all_gather(step_rows, 'vocab', axis=1, tiled=True)  35 us
    all_gather x1, blocking collectives, local(): joint_all = lax.all_gather(joint_rows, 'vocab', axis=0, tiled=True)  34.2 us
    gather x1, local copies, waits for them, and re-layouts, encode_local(): emb = phrase_table[ids]  20.2 us
  transfers between devices with their start and end apart: 3, of which 3 were waited for; matrix products, arithmetic and copies ran while one was open for 5% of the time, Pallas kernels for 0%

commit v1 on v0

--- a/solution.py
+++ b/solution.py
@@ -62,7 +62,12 @@
     keys = jnp.dot(phrase_vec, key_w, preferred_element_type=jnp.float32).astype(jnp.bfloat16)
     values = jnp.dot(phrase_vec, value_w, preferred_element_type=jnp.float32).astype(jnp.bfloat16)
     queries = jnp.dot(frames, query_w, preferred_element_type=jnp.float32).astype(jnp.bfloat16)
-    asked = lax.all_gather(queries, ("phrase", "vocab"), axis=0, tiled=True)
+    asked = jnp.concatenate(
+        lax.all_to_all(
+            jnp.stack([queries] * lax.axis_size(("phrase", "vocab"))), ("phrase", "vocab"), 0, 0
+        ),
+        axis=0,
+    )
     block_peak, block_total, block_numer = block_sums(asked, keys, values, 1)
     peak = lax.pmax(jnp.max(block_peak, -1), ("phrase", "vocab"))
     total, numer = rescale(block_peak, block_total, block_numer, peak)

time: 753 us -> 491 us (0.65)
  waiting for transfers between devices: 394 us -> 122 us
  starting transfers between devices: 0.3 us -> 11.8 us
    all_gather x1 -> x0, waiting for transfers between devices: 274 us -> none  [local(): asked = lax.all_gather(queries, ('phrase', 'vocab'), axis=0, tiled=True)]
    all_to_all x0 -> x1, starting transfers between devices: none -> 11.7 us  [local(): lax.all_to_all(jnp.stack([queries] * lax.axis_size(('phrase', 'vocab'))),...]
    unnamed x5 -> x4, waiting for transfers between devices: 120 us -> 121 us
  transfers between devices with their start and end apart: 3 -> 3, of which waited for: 3 -> 3; matrix products, arithmetic and copies ran while one was open for 5% -> 8% of each run, Pallas kernels for 0% -> 0%
where the time goes in v1:
time: 491 us; the launch traced here: 490 us
  blocking collectives  238 us (48%)
  waiting for transfers between devices  122 us (25%)
  local copies, waits for them, and re-layouts  48.1 us (10%)
  matrix products  36.1 us (7%)
  other arithmetic  19.1 us (4%)
  between operations  15.1 us (3%)
  starting transfers between devices  11.8 us (2%)
    unnamed x4, waiting for transfers between devices  121 us
    pmax x1, blocking collectives, local(): peak = lax.pmax(jnp.max(block_peak, -1), ('phrase', 'vocab'))  66.1 us
    unnamed x1, blocking collectives  62.9 us
    pmax x1, blocking collectives, local(): peak_rows = lax.pmax(jnp.max(logits, -1), 'vocab')  40.3 us
    all_gather x1, blocking collectives, local(): step_all = lax.all_gather(step_rows, 'vocab', axis=1, tiled=True)  34.7 us
    all_gather x1, blocking collectives, local(): joint_all = lax.all_gather(joint_rows, 'vocab', axis=0, tiled=True)  34.5 us
    gather x1, local copies, waits for them, and re-layouts, encode_local(): emb = phrase_table[ids]  20.2 us
    all_to_all x1, starting transfers between devices, local(): lax.all_to_all(jnp.stack([queries] * lax.axis_size(('phrase', 'vocab'))),...  11.7 us
  transfers between devices with their start and end apart: 3, of which 3 were waited for; matrix products, arithmetic and copies ran while one was open for 8% of the time, Pallas kernels for 0%

profile of v1, /device:TPU:0, one launch (start us, length us, event | category | flops | bytes accessed | tf_op | source)
XLA Modules:
  0.0 490.4 jit_solution(4134264136174751395)
XLA Ops:
  7.2 1.6 convolution_convert_fusion.3
  8.8 1.6 stack.2
  10.4 11.7 %all-to-all-start = ((bf16[128,12,512]{2,1,0:T(8,128)(2,1)}), bf16[128,12,512]{2,1,0:T(8,128)(2,1)}, u32[]{:S(2)}, u32[]{:S(2)}) async-start(bf16[128,12,512]{2,1,0:T(8,128)(2,1)} %stack.2), calls=%async_computation | async-start | bytes 4194304 | tf_op jit(solution)/shard_map/all_to_all | solution.py:66
  22.1 0.7 compare_select_fusion
  23.0 0.2 reshape.179
  23.4 20.2 %gather_fusion = bf16[4096,512]{1,0:T(8,128)(2,1)} fusion(bf16[4096,512]{1,0:T(8,128)(2,1)} %param.22, s32[4096]{0:T(1024)S(1)} %broadcast_clamp_fusion), kind=kCustom, calls=%fused_computation | custom fusion | bytes 8404992 | tf_op jit(solution)/shard_map/gather | solution.py:11
  43.6 0.1 fusion.22
  43.7 3.5 fusion.2
  47.2 0.5 fusion.8
  47.7 0.5 convolution_convert_fusion
  48.2 1.3 convolution_convert_fusion.1
  49.5 1.2 all-to-all-done
  50.7 3.2 reshape_reshape.3
  53.9 6.4 %bitcast_reduce_fusion = (f32[1536,4]{0,1:T(4,128)S(1)}, f32[4,512,1536]{2,1,0:T(8,128)}) fusion(bf16[512,4,128]{0,2,1:T(8,128)(2,1)S(1)} %bitcast.73, bf16[1536,4,128]{2,1,0:T(4,128)(2,1)S(1)} %reshape_reshape.3), kind=kOutput, calls=%fused_computation.4 | convolution fusion | flops 811591680 | bytes 14704640 | tf_op jit(solution)/shard_map/fhd,phd->fhp/dot_general | solution.py:24
  60.4 66.1 %pmax.14 = f32[1536,4]{0,1:T(4,128)S(1)} all-reduce(f32[1536,4]{0,1:T(4,128)S(1)} %get-tuple-element.19), channel_id=1, replica_groups=mesh['phrase'=16,'vocab'=8] {'phrase','vocab'}, use_global_device_ids=true, to_apply=%region_3.0 | all-reduce | flops 6144 | bytes 49152 | tf_op jit(solution)/shard_map/pmax | solution.py:72
  126.5 6.8 %convert_reduce_fusion = f32[1536,4]{0,1:T(4,128)S(1)} fusion(f32[1536,4]{0,1:T(4,128)S(1)} %get-tuple-element.19, f32[4,512,1536]{2,1,0:T(8,128)} %get-tuple-element.20), kind=kLoop, calls=%fused_computation.9 | loop fusion | flops 15722496 | bytes 12632064 | tf_op jit(solution)/shard_map/reduce_sum | solution.py:30
  133.3 0.6 fusion.36
  133.9 0.7 copy-done.1
  134.6 5.0 %fusion.5 = f32[1536,4,128]{0,2,1:T(8,128)} fusion(bf16[512,4,128]{0,2,1:T(8,128)(2,1)} %bitcast.74, f32[1536,4]{0,1:T(4,128)S(1)} %get-tuple-element.16, f32[4,512,1536]{2,1,0:T(8,128)S(1)} %copy-done.1, f32[1536,4]{0,1:T(4,128)S(1)} %get-tuple-element.19), kind=kOutput, calls=%fused_computation.14 | convolution fusion | flops 815529984 | bytes 16302080 | tf_op jit(solution)/shard_map/fhbp,bphd->fhbd/dot_general | solution.py:32
  139.7 5.0 %copy.47 = f32[1536,4,128]{2,1,0:T(4,128)} copy(f32[1536,4,128]{0,2,1:T(8,128)} %fusion.5) | data formatting | bytes 6291456 | tf_op jit(solution)/shard_map/reduce_sum | solution.py:40
  144.8 3.8 gather_fusion.1
  148.6 0.2 fusion.10
  148.9 34.7 %all_gather.7 = bf16[4,64,640]{2,0,1:T(4,128)(2,1)S(1)} all-gather(bf16[4,8,640]{2,0,1:T(4,128)(2,1)S(1)} %copy.49), channel_id=1, replica_groups=mesh['phrase'=16,'vocab'=8] {'vocab'}, dimensions={1}, use_global_device_ids=true | all-gather | bytes 368640 | tf_op jit(solution)/shard_map/all_gather | solution.py:97
  183.8 0.5 copy-done.10
  184.3 0.7 select_reduce_fusion.1
  185.0 0.8 copy.51
  185.8 0.7 eq.42
  186.5 1.2 dynamic-slice.2
  188.4 0.8 select_reduce_fusion.3
  189.2 0.9 convolution_reduce_fusion
  190.1 62.9 %all-reduce.1 = f32[1536,4]{0,1:T(4,128)S(1)} all-reduce(f32[1536,4]{0,1:T(4,128)} %get-tuple-element.15), channel_id=3, replica_groups=mesh['phrase'=16,'vocab'=8] {'phrase','vocab'}, use_global_device_ids=true, to_apply=%region_6.0.clone | all-reduce | flops 6144 | bytes 49152
  253.2 43.2 %all-reduce.8.cloned.1.call-done = f32[1536,4,128]{2,1,0:T(4,128)} async-done(((f32[1536,4,128]{2,1,0:T(4,128)}), f32[1536,4,128]{2,1,0:T(4,128)}) %all-reduce.8.cloned.1.call-update) | async-done | bytes 3145744
  296.3 0.8 fusion.27
  297.2 1.2 fusion.13
  298.4 34.5 %all-gather = bf16[8,12,640]{2,1,0:T(8,128)(2,1)S(1)} all-gather(bf16[1,12,640]{2,1,0:T(8,128)(2,1)S(1)} %fusion.13), channel_id=1, replica_groups=mesh['phrase'=16,'vocab'=8] {'vocab'}, dimensions={0}, use_global_device_ids=true | all-gather | bytes 138240 | tf_op jit(solution)/shard_map/all_gather | solution.py:85
  332.9 3.6 tanh_convert_fusion
  336.5 6.0 %copy.50 = bf16[96,64,640]{2,1,0:T(8,128)(2,1)} copy(bf16[96,64,640]{2,0,1:T(8,128)(2,1)S(1)} %tanh_convert_fusion) | data formatting | bytes 15728640 | tf_op jit(solution)/shard_map/convert_element_type | solution.py:115
  342.6 11.2 %fusion.37 = (f32[6144]{0:T(1024)S(1)}, f32[6144,512]{0,1:T(8,128)}) fusion(bf16[6144,640]{1,0:T(8,128)(2,1)} %bitcast.72, bf16[640,512]{1,0:T(8,128)(2,1)S(1)} %copy-done.11), kind=kOutput, calls=%fused_computation.74 | convolution fusion | flops 4029671424 | bytes 21127168 | tf_op jit(solution)/shard_map/dot_general | solution.py:118
  353.8 40.3 %pmax.15 = f32[6144]{0:T(1024)S(1)} all-reduce(f32[6144]{0:T(1024)S(1)} %get-tuple-element.21), channel_id=1, replica_groups=mesh['phrase'=16,'vocab'=8] {'vocab'}, use_global_device_ids=true, to_apply=%region_9.10 | all-reduce | flops 6144 | bytes 49152 | tf_op jit(solution)/shard_map/pmax | solution.py:127
  394.2 6.5 %select_reduce_fusion = (f32[6144]{0:T(1024)S(1)}, f32[6144]{0:T(1024)S(1)}) fusion(f32[6144,512]{0,1:T(8,128)} %get-tuple-element.22, s32[6144]{0:T(1024)S(1)} %copy-done.6, s32[512]{0:T(512)S(1)} %iota_add_fusion, f32[6144]{0:T(1024)S(1)} %pmax.15), kind=kLoop, calls=%fused_computation.7 | loop fusion | flops 15716352 | bytes 12683264 | tf_op jit(solution)/shard_map/reduce_sum | solution.py:122
  400.7 0.7 reshape.175
  401.4 0.7 reshape.176
  402.1 1.0 fusion.26
  403.1 0.7 select_n.81
  403.9 77.4 %all-reduce.10.cloned.1.call-done = (f32[96,64]{1,0:T(8,128)}, f32[96,64]{1,0:T(8,128)}, f32[96,64]{1,0:T(8,128)}) async-done(((f32[96,64]{1,0:T(8,128)}, f32[96,64]{1,0:T(8,128)}, f32[96,64]{1,0:T(8,128)}), (f32[96,64]{1,0:T(8,128)}, f32[96,64]{1,0:T(8,128)}, f32[96,64]{1,0:T(8,128)})) %all-reduce.10.cloned.1.call-update) | async-done | bytes 73744
  481.2 1.0 fusion.24
  482.2 0.7 copy.52
  482.9 0.7 copy.53
  (49 shorter events, 1.0 us)
Async XLA Ops:
  7.2 290.0 %copy-start = (bf16[1024,640]{1,0:T(8,128)(2,1)S(1)}, bf16[1024,640]{1,0:T(8,128)(2,1)}, u32[]{:S(2)}) copy-start(bf16[1024,640]{1,0:T(8,128)(2,1)} %param.28) | copy-start | bytes 3932164
  7.2 16.0 %copy-start.7 = (s32[512]{0:T(512)S(1)}, s32[512]{0:T(512)}, u32[]{:S(2)}) copy-start(s32[512]{0:T(512)} %param.21) | copy-start | bytes 6148
  7.2 16.0 %copy-start.8 = (s32[4,64]{1,0:T(4,128)S(1)}, s32[4,64]{1,0:T(4,128)}, u32[]{:S(2)}) copy-start(s32[4,64]{1,0:T(4,128)} %param.18) | copy-start | bytes 3076
  10.4 40.3 %all-to-all-start = ((bf16[128,12,512]{2,1,0:T(8,128)(2,1)}), bf16[128,12,512]{2,1,0:T(8,128)(2,1)}, u32[]{:S(2)}, u32[]{:S(2)}) async-start(bf16[128,12,512]{2,1,0:T(8,128)(2,1)} %stack.2), calls=%async_computation | async-start | bytes 4194304 | tf_op jit(solution)/shard_map/all_to_all | solution.py:66
  22.1 274.2 %all-reduce.8.cloned.1.call-start = ((), (), s32[]{:S(2)}) async-start(), calls=%async_computation.1 | async-start | bytes 6291456
  23.4 23.8 %copy-start.12 = (bf16[512,512]{1,0:T(8,128)(2,1)S(1)}, bf16[512,512]{1,0:T(8,128)(2,1)}, u32[]{:S(2)}) copy-start(bf16[512,512]{1,0:T(8,128)(2,1)} %param.23) | copy-start | bytes 1572868
  43.5 4.2 copy-start.4
  43.5 4.7 copy-start.5
  126.5 8.2 %copy-start.1 = (f32[4,512,1536]{2,1,0:T(8,128)S(1)}, f32[4,512,1536]{2,1,0:T(8,128)}, u32[]{:S(2)}) copy-start(f32[4,512,1536]{2,1,0:T(8,128)} %get-tuple-element.20) | copy-start | bytes 37748740
  139.7 8.9 %copy-start.2 = (bf16[640,640]{1,0:T(8,128)(2,1)S(1)}, bf16[640,640]{1,0:T(8,128)(2,1)}, u32[]{:S(2)}) copy-start(bf16[640,640]{1,0:T(8,128)(2,1)} %param.30) | copy-start | bytes 2457604
  139.7 48.7 %copy-start.9 = (s32[4]{0:T(128)S(1)}, s32[4]{0:T(128)}, u32[]{:S(2)}) copy-start(s32[4]{0:T(128)} %param.17) | copy-start | bytes 52
  139.7 157.5 %copy-start.3 = (bf16[512,1024]{1,0:T(8,128)(2,1)S(1)}, bf16[512,1024]{1,0:T(8,128)(2,1)}, u32[]{:S(2)}) copy-start(bf16[512,1024]{1,0:T(8,128)(2,1)} %param.27) | copy-start | bytes 3145732
  144.7 336.6 %all-reduce.10.cloned.1.call-start = ((), (), s32[]{:S(2)}) async-start(), calls=%async_computation.2 | async-start | bytes 294912
  183.7 0.5 copy-start.10
  336.5 6.0 %copy-start.11 = (bf16[640,512]{1,0:T(8,128)(2,1)S(1)}, bf16[640,512]{1,0:T(8,128)(2,1)}, u32[]{:S(2)}) copy-start(bf16[640,512]{1,0:T(8,128)(2,1)} %param.31) | copy-start | bytes 1966084
  342.6 51.6 %copy-start.6 = (s32[6144]{0:T(1024)S(1)}, s32[6144]{0:T(1024)}, u32[]{:S(2)}) copy-start(s32[6144]{0:T(1024)} %eq.42) | copy-start | bytes 73732
Sparse Core Ops, SparseCore 0:
  144.8 151.4 all-reduce.7
  403.9 77.2 all-reduce.9
